TPU v7x, 32 devices: a whole 2x2x4 slice. The times are simulated.
32 devices in a mesh: dp: 8 (over y, x, core), tp: 4 (over z).
Axes of the slice: x: 2, y: 2, z: 4, core: 2. Of those that a mesh axis runs over, the one named last changes fastest.
Arguments:
- tokens: bfloat16 [16384, 2048], P('dp'), may hold values from -6 to 6
- doc_ids: int32 [16, 1024], P('dp'), may hold values from 0 to 3, never falling along the last dimension, each value on 1 to 512 neighbouring positions
- norm1_gain: bfloat16 [2048], replicated, may hold values from 0.5 to 1.5
- norm1_bias: bfloat16 [2048], replicated, may hold values from -4 to 4
- query_weight: bfloat16 [2048, 2048], P(None, 'tp'), may hold values from -0.125 to 0.125
- query_bias: bfloat16 [2048], P('tp'), may hold values from -6 to 6
- keyval_weight: bfloat16 [2048, 256], replicated, may hold values from -0.125 to 0.125
- value_bias: bfloat16 [128], replicated, may hold values from -3 to 3
- out_weight: bfloat16 [2048, 2048], P('tp'), may hold values from -0.5 to 0.5
- out_bias: bfloat16 [2048], replicated, may hold values from -6 to 6
- norm2_gain: bfloat16 [2048], replicated, may hold values from 0.5 to 1.5
- norm2_bias: bfloat16 [2048], replicated, may hold values from -4 to 4
- up_weight: bfloat16 [2048, 8192], P(None, 'tp'), may hold values from -0.125 to 0.125
- up_bias: bfloat16 [8192], P('tp'), may hold values from -6 to 6
- down_weight: bfloat16 [8192, 2048], P('tp'), may hold values from -0.0625 to 0.0625
- down_bias: bfloat16 [2048], replicated, may hold values from -6 to 6
- grad_out: bfloat16 [16384, 2048], P('dp'), may hold values from -6 to 6
Outputs:
- output: bfloat16 [16384, 2048], P('dp')
- grad_tokens: bfloat16 [16384, 2048], P('dp')
- grad_norm1_gain: float32 [2048], P('dp')
- grad_norm1_bias: float32 [2048], P('dp')
- grad_query_weight: float32 [2048, 2048], P('dp', 'tp')
- grad_query_bias: float32 [2048], P(('tp', 'dp'))
- grad_keyval_weight: float32 [2048, 256], P(('dp', 'tp'))
- grad_value_bias: float32 [128], P(('dp', 'tp'))
- grad_out_weight: float32 [2048, 2048], P('tp', 'dp')
- grad_out_bias: float32 [2048], P('dp')
- grad_norm2_gain: float32 [2048], P('dp')
- grad_norm2_bias: float32 [2048], P('dp')
- grad_up_weight: float32 [2048, 8192], P('dp', 'tp')
- grad_up_bias: float32 [8192], P(('tp', 'dp'))
- grad_down_weight: float32 [8192, 2048], P('tp', 'dp')
- grad_down_bias: float32 [2048], P('dp')
Inputs may be any that keep to these rules, and one draw needn't show every extreme that they name: `doc_ids`: document numbers never fall along a row of a window; a document spans 1 to half of 1024 tokens.
All inputs are finite; a program needn't handle non-finite values.
Results may differ from a plain program's by a relative error of at most 0.02.
Values may be sent and summed in bfloat16 or wider, within the bound.
A program may use at most 384 MiB of HBM per device.

v0:
```python
import jax
import jax.numpy as jnp
from jax import lax
from jax.sharding import PartitionSpec as P


def layer_norm(values, gain_vec, shift_vec):
    center = values - jnp.mean(values, axis=-1, keepdims=True)
    spread = jnp.mean(center * center, axis=-1, keepdims=True)
    return center * lax.rsqrt(spread + 1e-05) * gain_vec + shift_vec


def gelu_tanh(values):
    return jax.nn.gelu(values, approximate=True)


def allowed_mask(doc_row):
    places = jnp.arange(doc_row.shape[0])
    return (doc_row[:, None] == doc_row[None, :]) & (places[:, None] >= places[None, :])


def masked_scores(heads_q, keys_low, allowed, score_scale):
    scores = (
        jnp.einsum("shd,td->hst", heads_q, keys_low, preferred_element_type=jnp.float32)
        * score_scale
    )
    return jnp.where(allowed[None], scores, -1e30)


def forward_block(seq_rows, doc_row, params, score_scale, head_dim):
    seq_len = seq_rows.shape[0]
    normed1 = layer_norm(seq_rows, params["norm1_gain"], params["norm1_bias"]).astype(jnp.bfloat16)
    queries = (
        jnp.dot(normed1, params["query_weight"], preferred_element_type=jnp.float32)
        + params["query_bias"]
    )
    heads_q = queries.astype(jnp.bfloat16).reshape(seq_len, -1, head_dim)
    keyval = jnp.dot(normed1, params["keyval_weight"], preferred_element_type=jnp.float32)
    keys_low = keyval[:, :head_dim].astype(jnp.bfloat16)
    values_low = (keyval[:, head_dim:] + params["value_bias"]).astype(jnp.bfloat16)
    allowed = allowed_mask(doc_row)
    scores = masked_scores(heads_q, keys_low, allowed, score_scale)
    highest = jnp.max(scores, axis=2, keepdims=True)
    lifted = jnp.exp(scores - highest)
    totals = jnp.sum(lifted, axis=2, keepdims=True)
    chances = lifted / totals
    log_totals = (highest + jnp.log(totals))[..., 0]
    attended = (
        jnp.einsum(
            "hst,td->shd",
            chances.astype(jnp.bfloat16),
            values_low,
            preferred_element_type=jnp.float32,
        )
        .astype(jnp.bfloat16)
        .reshape(seq_len, -1)
    )
    partial_value = jnp.dot(attended, params["out_weight"], preferred_element_type=jnp.float32)
    mixed_sum = lax.psum(partial_value.astype(jnp.bfloat16), "tp").astype(jnp.float32)
    hidden1 = seq_rows + mixed_sum + params["out_bias"]
    normed2 = layer_norm(hidden1, params["norm2_gain"], params["norm2_bias"]).astype(jnp.bfloat16)
    before = (
        jnp.dot(normed2, params["up_weight"], preferred_element_type=jnp.float32)
        + params["up_bias"]
    )
    activated = gelu_tanh(before).astype(jnp.bfloat16)
    down_part = jnp.dot(activated, params["down_weight"], preferred_element_type=jnp.float32)
    summed = lax.psum(down_part.astype(jnp.bfloat16), "tp").astype(jnp.float32)
    result = hidden1 + summed + params["down_bias"]
    kept_state = (
        normed1,
        heads_q,
        keys_low,
        values_low,
        allowed,
        log_totals,
        attended,
        hidden1,
        normed2,
        before,
        activated,
    )
    return (result, kept_state)


def backward_block(seq_rows, cotangent, kept_state, params, score_scale, head_dim):
    (
        normed1,
        heads_q,
        keys_low,
        values_low,
        allowed,
        log_totals,
        attended,
        hidden1,
        normed2,
        before,
        activated,
    ) = kept_state
    seq_len = seq_rows.shape[0]
    grad_low = cotangent.astype(jnp.bfloat16)
    grad_down_bias = jnp.sum(cotangent, axis=0)
    grad_down_weight = jnp.dot(activated.T, grad_low, preferred_element_type=jnp.float32)
    grad_activated = jnp.dot(grad_low, params["down_weight"].T, preferred_element_type=jnp.float32)
    grad_before = jax.vjp(gelu_tanh, before)[1](grad_activated)[0].astype(jnp.bfloat16)
    grad_up_weight = jnp.dot(normed2.T, grad_before, preferred_element_type=jnp.float32)
    grad_up_bias = jnp.sum(grad_before.astype(jnp.float32), axis=0)
    partial2 = jnp.dot(grad_before, params["up_weight"].T, preferred_element_type=jnp.float32)
    grad_normed2 = lax.psum(partial2.astype(jnp.bfloat16), "tp").astype(jnp.float32)
    norm2_pull = jax.vjp(layer_norm, hidden1, params["norm2_gain"], params["norm2_bias"])[1]
    through2, grad_norm2_gain, grad_norm2_bias = norm2_pull(grad_normed2)
    grad_hidden1 = cotangent + through2
    grad_out_bias = jnp.sum(grad_hidden1, axis=0)
    grad_mixed = grad_hidden1.astype(jnp.bfloat16)
    grad_out_weight = jnp.dot(attended.T, grad_mixed, preferred_element_type=jnp.float32)
    grad_attended = jnp.dot(grad_mixed, params["out_weight"].T, preferred_element_type=jnp.float32)
    grad_attended = grad_attended.astype(jnp.bfloat16).reshape(seq_len, -1, head_dim)
    scores = masked_scores(heads_q, keys_low, allowed, score_scale)
    chances = jnp.exp(scores - log_totals[..., None])
    grad_chances = jnp.einsum(
        "shd,td->hst", grad_attended, values_low, preferred_element_type=jnp.float32
    )
    grad_values = jnp.einsum(
        "hst,shd->td",
        chances.astype(jnp.bfloat16),
        grad_attended,
        preferred_element_type=jnp.float32,
    )
    weighted = jnp.sum(chances * grad_chances, axis=2, keepdims=True)
    grad_scores = (chances * (grad_chances - weighted) * score_scale).astype(jnp.bfloat16)
    grad_queries = jnp.einsum(
        "hst,td->shd", grad_scores, keys_low, preferred_element_type=jnp.float32
    )
    grad_queries = grad_queries.reshape(seq_len, -1).astype(jnp.bfloat16)
    grad_keys = jnp.einsum("hst,shd->td", grad_scores, heads_q, preferred_element_type=jnp.float32)
    grad_keyval = jnp.concatenate([grad_keys, grad_values], axis=1).astype(jnp.bfloat16)
    grad_query_weight = jnp.dot(normed1.T, grad_queries, preferred_element_type=jnp.float32)
    grad_query_bias = jnp.sum(grad_queries.astype(jnp.float32), axis=0)
    grad_keyval_weight = jnp.dot(normed1.T, grad_keyval, preferred_element_type=jnp.float32)
    grad_value_bias = jnp.sum(grad_keyval[:, head_dim:].astype(jnp.float32), axis=0)
    partial1 = jnp.dot(grad_queries, params["query_weight"].T, preferred_element_type=jnp.float32)
    partial1 = partial1 + jnp.dot(
        grad_keyval, params["keyval_weight"].T, preferred_element_type=jnp.float32
    )
    grad_normed1 = lax.psum(partial1.astype(jnp.bfloat16), "tp").astype(jnp.float32)
    norm1_pull = jax.vjp(layer_norm, seq_rows, params["norm1_gain"], params["norm1_bias"])[1]
    through1, grad_norm1_gain, grad_norm1_bias = norm1_pull(grad_normed1)
    grad_input = grad_hidden1 + through1
    grad_terms = (
        grad_query_weight,
        grad_up_weight,
        grad_query_bias,
        grad_up_bias,
        grad_norm1_gain,
        grad_norm1_bias,
        grad_out_bias,
        grad_norm2_gain,
        grad_norm2_bias,
        grad_down_bias,
        grad_out_weight,
        grad_down_weight,
        grad_keyval_weight,
        grad_value_bias,
    )
    return (grad_input, grad_terms)


def reduce_once(grad_terms):
    row_shards = (
        lax.psum_scatter(
            grad_terms[0].astype(jnp.bfloat16), "dp", scatter_dimension=0, tiled=True
        ).astype(jnp.float32),
        lax.psum_scatter(
            grad_terms[1].astype(jnp.bfloat16), "dp", scatter_dimension=0, tiled=True
        ).astype(jnp.float32),
        lax.psum_scatter(
            grad_terms[2].astype(jnp.bfloat16), "dp", scatter_dimension=0, tiled=True
        ).astype(jnp.float32),
        lax.psum_scatter(
            grad_terms[3].astype(jnp.bfloat16), "dp", scatter_dimension=0, tiled=True
        ).astype(jnp.float32),
        lax.psum_scatter(
            grad_terms[4].astype(jnp.bfloat16), "dp", scatter_dimension=0, tiled=True
        ).astype(jnp.float32),
        lax.psum_scatter(
            grad_terms[5].astype(jnp.bfloat16), "dp", scatter_dimension=0, tiled=True
        ).astype(jnp.float32),
        lax.psum_scatter(
            grad_terms[6].astype(jnp.bfloat16), "dp", scatter_dimension=0, tiled=True
        ).astype(jnp.float32),
        lax.psum_scatter(
            grad_terms[7].astype(jnp.bfloat16), "dp", scatter_dimension=0, tiled=True
        ).astype(jnp.float32),
        lax.psum_scatter(
            grad_terms[8].astype(jnp.bfloat16), "dp", scatter_dimension=0, tiled=True
        ).astype(jnp.float32),
        lax.psum_scatter(
            grad_terms[9].astype(jnp.bfloat16), "dp", scatter_dimension=0, tiled=True
        ).astype(jnp.float32),
    )
    col_shards = (
        lax.psum_scatter(
            grad_terms[10].astype(jnp.bfloat16), "dp", scatter_dimension=1, tiled=True
        ).astype(jnp.float32),
        lax.psum_scatter(
            grad_terms[11].astype(jnp.bfloat16), "dp", scatter_dimension=1, tiled=True
        ).astype(jnp.float32),
    )
    shared_shards = (
        lax.psum_scatter(grad_terms[12], ("dp", "tp"), scatter_dimension=0, tiled=True),
        lax.psum_scatter(grad_terms[13], ("dp", "tp"), scatter_dimension=0, tiled=True),
    )
    return tuple(row_shards) + tuple(col_shards) + tuple(shared_shards)


def per_device(
    tokens,
    doc_ids,
    norm1_gain,
    norm1_bias,
    query_weight,
    query_bias,
    keyval_weight,
    value_bias,
    out_weight,
    out_bias,
    norm2_gain,
    norm2_bias,
    up_weight,
    up_bias,
    down_weight,
    down_bias,
    grad_out,
):
    micro_count = doc_ids.shape[0]
    seq_len = doc_ids.shape[1]
    head_dim = value_bias.shape[0]
    score_scale = head_dim ** (-0.5)
    params = {
        "norm1_gain": norm1_gain.astype(jnp.float32),
        "norm1_bias": norm1_bias.astype(jnp.float32),
        "query_weight": query_weight,
        "query_bias": query_bias.astype(jnp.float32),
        "keyval_weight": keyval_weight,
        "value_bias": value_bias.astype(jnp.float32),
        "out_weight": out_weight,
        "out_bias": out_bias.astype(jnp.float32),
        "norm2_gain": norm2_gain.astype(jnp.float32),
        "norm2_bias": norm2_bias.astype(jnp.float32),
        "up_weight": up_weight,
        "up_bias": up_bias.astype(jnp.float32),
        "down_weight": down_weight,
        "down_bias": down_bias.astype(jnp.float32),
    }
    results = []
    input_grads = []
    running = None
    for micro_index in range(micro_count):
        seq_rows = tokens[micro_index * seq_len : (micro_index + 1) * seq_len].astype(jnp.float32)
        cotangent = grad_out[micro_index * seq_len : (micro_index + 1) * seq_len].astype(
            jnp.float32
        )
        result, kept_state = forward_block(
            seq_rows, doc_ids[micro_index], params, score_scale, head_dim
        )
        results.append(result.astype(jnp.bfloat16))
        grad_input, grad_terms = backward_block(
            seq_rows, cotangent, kept_state, params, score_scale, head_dim
        )
        input_grads.append(grad_input.astype(jnp.bfloat16))
        if running is None:
            running = grad_terms
        else:
            running = tuple((current + incoming for current, incoming in zip(running, grad_terms)))
    running = reduce_once(running)
    return (
        jnp.concatenate(results, axis=0),
        jnp.concatenate(input_grads, axis=0),
        running[4],
        running[5],
        running[0],
        running[2],
        running[12],
        running[13],
        running[10],
        running[6],
        running[7],
        running[8],
        running[1],
        running[3],
        running[11],
        running[9],
    )


def solution(mesh):
    return jax.shard_map(
        per_device,
        mesh=mesh,
        in_specs=(
            P("dp", None),
            P("dp", None),
            P(),
            P(),
            P(None, "tp"),
            P("tp"),
            P(),
            P(),
            P("tp", None),
            P(),
            P(),
            P(),
            P(None, "tp"),
            P("tp"),
            P("tp", None),
            P(),
            P("dp", None),
        ),
        out_specs=(
            P("dp", None),
            P("dp", None),
            P("dp"),
            P("dp"),
            P("dp", "tp"),
            P(("tp", "dp")),
            P(("dp", "tp"), None),
            P(("dp", "tp")),
            P("tp", "dp"),
            P("dp"),
            P("dp"),
            P("dp"),
            P("dp", "tp"),
            P(("tp", "dp")),
            P("tp", "dp"),
            P("dp"),
        ),
        check_vma=False,
    )
```

profile of v0, /device:TPU:0, one launch (start us, length us, event | category | flops | bytes accessed | tf_op | source)
XLA Modules:
  0.0 1856.1 jit_solution(11825210403797541873)
XLA Ops:
  53.8 157.1 %all-reduce.17.cloned.1.call-done = bf16[1024,2048]{1,0:T(8,128)(2,1)} async-done(((bf16[1024,2048]{1,0:T(8,128)(2,1)}), bf16[1024,2048]{1,0:T(8,128)(2,1)}) %all-reduce.17.cloned.1.call-update) | async-done | bytes 4194320 | tf_op jit(solution)/shard_map/psum | solution.py:59
  254.4 154.0 %all-reduce.19.cloned.1.call-done = bf16[1024,2048]{1,0:T(8,128)(2,1)} async-done(((bf16[1024,2048]{1,0:T(8,128)(2,1)}), bf16[1024,2048]{1,0:T(8,128)(2,1)}) %all-reduce.19.cloned.1.call-update) | async-done | bytes 4194320 | tf_op jit(solution)/shard_map/psum | solution.py:59
  408.4 8.8 multiply_reduce_fusion.1
  421.3 15.1 fusion.162
  436.4 21.1 %convert_reduce_fusion.8 = (f32[2048]{0:T(1024)}, bf16[1024,2048]{1,0:T(8,128)(2,1)}) fusion(f32[1024,2048]{1,0:T(8,128)} %fusion.162, f32[2048]{0:T(1024)S(1)} %convert_element_type.317, bf16[2048,2048]{1,0:T(8,128)(2,1)} %param.31, bf16[2048,2048]{1,0:T(8,128)(2,1)} %param.33), kind=kOutput, calls=%fused_computation.106 | convolution fusion | flops 8638167040 | bytes 25182208 | tf_op jit(solution)/shard_map/dot_general | solution.py:104
  457.5 14.1 convolution_convert_fusion
  471.6 13.9 fusion.161
  485.5 19.2 %convert_reduce_fusion.9 = (f32[2048]{0:T(1024)}, bf16[1024,2048]{1,0:T(8,128)(2,1)S(1)}) fusion(f32[1024,2048]{1,0:T(8,128)} %fusion.161, f32[2048]{0:T(1024)S(1)} %convert_element_type.317, bf16[2048,2048]{1,0:T(8,128)(2,1)} %param.31, bf16[2048,2048]{1,0:T(8,128)(2,1)} %param.33), kind=kOutput, calls=%fused_computation.107 | convolution fusion | flops 8638167040 | bytes 25182208 | tf_op jit(solution)/shard_map/dot_general | solution.py:104
  506.6 12.8 convolution_convert_fusion.1
  520.2 289.9 %all-reduce.23.cloned.1.call-done = (bf16[1024,2048]{1,0:T(8,128)(2,1)}, bf16[1024,2048]{1,0:T(8,128)(2,1)}) async-done(((bf16[1024,2048]{1,0:T(8,128)(2,1)}, bf16[1024,2048]{1,0:T(8,128)(2,1)}), (bf16[1024,2048]{1,0:T(8,128)(2,1)}, bf16[1024,2048]{1,0:T(8,128)(2,1)})) %all-reduce.23.cloned.1.call-update) | async-done | bytes 8388624 | tf_op jit(solution)/shard_map/psum | solution.py:109
  810.2 12.3 fusion.33
  823.3 12.4 fusion.54
  835.7 14.1 fusion.168
  863.5 9.8 fusion.135
  873.3 26.1 %convert_reduce_fusion.10 = (f32[128,4]{0,1:T(4,128)}, bf16[128,4,1024]{2,0,1:T(8,128)(2,1)}) fusion(f32[1024,1024,4]{1,0,2:T(8,128)} %fusion.135, f32[4,1024,1024]{1,2,0:T(8,128)} %get-tuple-element.75, f32[4,1024]{1,0:T(4,128)S(1)} %log_add_fusion, f32[1024,256]{1,0:T(8,128)} %copy-done.32), kind=kOutput, calls=%fused_computation.155 | convolution fusion | flops 1104679424 | bytes 68454400 | tf_op jit(solution)/shard_map/hst,td->shd/dot_general | solution.py:131
  914.4 24.0 %convert_reduce_fusion.11 = (f32[128,4]{0,1:T(4,128)}, bf16[128,4,1024]{2,0,1:T(8,128)(2,1)S(1)}) fusion(f32[1024,1024,4]{1,0,2:T(8,128)} %fusion.138, f32[4,1024,1024]{1,2,0:T(8,128)} %get-tuple-element.73, f32[4,1024]{1,0:T(4,128)S(1)} %log_add_fusion.1, f32[1024,256]{1,0:T(8,128)S(1)} %copy-done.31), kind=kOutput, calls=%fused_computation.156 | convolution fusion | flops 1104679424 | bytes 68454400 | tf_op jit(solution)/shard_map/hst,td->shd/dot_general | solution.py:131
  947.2 20.6 %fusion.85 = f32[2048,2048]{1,0:T(8,128)} fusion(bf16[2048,2048]{1,0:T(8,128)(2,1)} %param.33, f32[1024,2048]{1,0:T(8,128)} %fusion.161, f32[2048]{0:T(1024)S(1)} %convert_element_type.317), kind=kOutput, calls=%fused_computation.150 | convolution fusion | flops 8610906112 | bytes 29368320 | tf_op jit(solution)/shard_map/dot_general | solution.py:103
  967.8 21.9 %add_convert_fusion = bf16[2048,2048]{1,0:T(8,128)(2,1)} fusion(f32[2048,2048]{1,0:T(8,128)} %fusion.85, bf16[2048,2048]{1,0:T(8,128)(2,1)} %param.33, f32[1024,2048]{1,0:T(8,128)} %fusion.162, f32[2048]{0:T(1024)S(1)} %convert_element_type.317), kind=kOutput, calls=%fused_computation.14 | convolution fusion | flops 8619294720 | bytes 37756928 | tf_op jit(solution)/shard_map/dot_general | solution.py:103
  990.4 17.5 fusion.160
  1007.9 17.5 add_convert_fusion.1
  1025.4 16.5 convolution_convert_fusion.2
  1041.9 16.0 convolution_convert_fusion.4
  1058.0 26.8 %fusion.123 = bf16[1024,128]{0,1:T(8,128)(2,1)S(1)} fusion(bf16[1024,4,128]{0,2,1:T(8,128)(2,1)S(1)} %bitcast.204, f32[1024,1024,4]{1,0,2:T(8,128)} %fusion.135, f32[4,1024,1024]{1,2,0:T(8,128)} %get-tuple-element.75, f32[4,1024]{1,0:T(4,128)S(1)} %copy-done.38), kind=kOutput, calls=%fused_computation.179 | convolution fusion | flops 1103238144 | bytes 34881536 | tf_op jit(solution)/shard_map/hst,shd->td/dot_general | solution.py:135
  1084.9 24.9 %fusion.122 = bf16[1024,128]{0,1:T(8,128)(2,1)S(1)} fusion(bf16[1024,4,128]{0,2,1:T(8,128)(2,1)S(1)} %bitcast.202, f32[1024,1024,4]{1,0,2:T(8,128)} %fusion.138, f32[4,1024,1024]{1,2,0:T(8,128)} %get-tuple-element.73, f32[4,1024]{1,0:T(4,128)S(1)} %copy-done.36), kind=kOutput, calls=%fused_computation.178 | convolution fusion | flops 1103238144 | bytes 34881536 | tf_op jit(solution)/shard_map/hst,shd->td/dot_general | solution.py:135
  1119.8 9.6 convert_reduce_fusion.12
  1151.2 43.5 %all-reduce.3 = f32[128]{0:T(128)S(1)} all-reduce(f32[128]{0:T(128)S(1)} %add.343), channel_id=7, replica_groups=mesh['dp'=8,'tp'=4] {'dp','tp'}, use_global_device_ids=true, to_apply=%region_43.44.clone | all-reduce | flops 128 | bytes 1024
  1213.1 496.3 %all-reduce.21.cloned.1.call-done = (bf16[1024,2048]{1,0:T(8,128)(2,1)}, bf16[1024,2048]{1,0:T(8,128)(2,1)}, bf16[1024,2048]{1,0:T(8,128)(2,1)}, bf16[1024,2048]{1,0:T(8,128)(2,1)}) async-done(((bf16[1024,2048]{1,0:T(8,128)(2,1)}, bf16[1024,2048]{1,0:T(8,128)(2,1)}, bf16[1024,2048]{1,0:T(8,128)(2,1)}, bf16[1024,2048]{1,0:T(8,128)(2,1)}), (bf16[1024,2048]{1,0:T(8,128)(2,1)}, bf16[1024,2048]{1,0:T(8,128)(2,1)}, ...) | async-done | bytes 16777232 | tf_op jit(solution)/shard_map/psum | solution.py:68
  1709.5 8.8 fusion.49
  1720.2 15.9 fusion.55
  1736.2 25.3 %all-reduce.9 = (bf16[2048]{0:T(1024)(128)(2,1)S(1)}, bf16[2048]{0:T(1024)(128)(2,1)S(1)}, bf16[512]{0:T(512)(128)(2,1)S(1)}, bf16[2048]{0:T(1024)(128)(2,1)S(1)...) all-reduce(bf16[2048]{0:T(1024)(128)(2,1)S(1)} %add_convert_fusion., ...), channel_id=2, replica_groups=mesh['dp'=8,'tp'=4] {'dp'}, use_global_device_ids=true, to_apply=%region_32.33.clone | all-reduce | flops 14848 | bytes 59392
  1766.5 16.8 add_convert_fusion.4
  1800.5 48.8 %reduce-scatter.8.cloned.1.call-done = f32[64,256]{1,0:T(8,128)} async-done(((f32[2048,256]{1,0:T(8,128)}), f32[64,256]{1,0:T(8,128)}) %reduce-scatter.8.cloned.1.call-update) | async-done | bytes 65552 | tf_op jit(solution)/shard_map/reduce_scatter | solution.py:210
  (304 shorter events, 207.9 us)
Async XLA Ops:
  7.2 41.4 %copy-start = (bf16[512,2048]{1,0:T(8,128)(2,1)S(1)}, bf16[512,2048]{1,0:T(8,128)(2,1)}, u32[]{:S(2)}) copy-start(bf16[512,2048]{1,0:T(8,128)(2,1)} %param.25) | copy-start | bytes 6291460
  7.2 203.7 %all-reduce.17.cloned.1.call-start = ((), (), s32[]{:S(2)}) async-start(), calls=%async_computation.5 | async-start | bytes 8388608 | tf_op jit(solution)/shard_map/psum | solution.py:59
  8.1 232.8 %copy-start.71 = (f32[128]{0:T(128)}, f32[128]{0:T(128)S(1)}, u32[]{:S(2)}) copy-start(f32[128]{0:T(128)S(1)} %convert_element_type.304) | copy-start | bytes 1540
  13.0 204.1 %copy-start.33 = (f32[2048]{0:T(1024)}, f32[2048]{0:T(1024)S(1)}, u32[]{:S(2)}) copy-start(f32[2048]{0:T(1024)S(1)} %convert_element_type.301) | copy-start | bytes 24580
  53.1 355.4 %all-reduce.19.cloned.1.call-start = ((), (), s32[]{:S(2)}) async-start(), calls=%async_computation.6 | async-start | bytes 8388608 | tf_op jit(solution)/shard_map/psum | solution.py:59
  53.2 168.5 %copy-start.41 = (f32[1024]{0:T(1024)}, f32[1024]{0:T(1024)S(1)}, u32[]{:S(2)}) copy-start(f32[1024]{0:T(1024)S(1)} %broadcast_multiply_fusion.1) | copy-start | bytes 12292
  254.3 555.9 %all-reduce.23.cloned.1.call-start = ((), (), s32[]{:S(2)}) async-start(), calls=%async_computation.13 | async-start | bytes 16777216 | tf_op jit(solution)/shard_map/psum | solution.py:109
  254.4 217.2 %copy-start.61 = (f32[2048]{0:T(1024)}, f32[2048]{0:T(1024)S(1)}, u32[]{:S(2)}) copy-start(f32[2048]{0:T(1024)S(1)} %convert_element_type.315) | copy-start | bytes 24580
  421.3 50.3 %slice-start = ((s8[8388608]{0:T(1024)(128)(4,1)}), s8[4194304]{0:T(1024)(128)(4,1)S(1)}, s32[]{:S(2)}) async-start(s8[8388608]{0:T(1024)(128)(4,1)} %bitcast.191), calls=%async_computation.14 | async-start | bytes 8388608
  436.4 35.2 %slice-start.1 = ((s8[8388608]{0:T(1024)(128)(4,1)}), s8[4194304]{0:T(1024)(128)(4,1)S(1)}, s32[]{:S(2)}) async-start(s8[8388608]{0:T(1024)(128)(4,1)} %bitcast.191), calls=%async_computation.15 | async-start | bytes 8388608
  519.5 684.5 %reduce-scatter.10.cloned.1.call-start = ((), (), s32[]{:S(2)}) async-start(), calls=%async_computation.9 | async-start | bytes 2359296 | tf_op jit(solution)/shard_map/reduce_scatter | solution.py:202
  520.2 394.2 %copy-start.35 = (f32[4,1024]{1,0:T(4,128)}, f32[4,1024]{1,0:T(4,128)S(1)}, u32[]{:S(2)}) copy-start(f32[4,1024]{1,0:T(4,128)S(1)} %log_add_fusion.1) | copy-start | bytes 49156
  520.2 353.1 %copy-start.37 = (f32[4,1024]{1,0:T(4,128)}, f32[4,1024]{1,0:T(4,128)S(1)}, u32[]{:S(2)}) copy-start(f32[4,1024]{1,0:T(4,128)S(1)} %log_add_fusion) | copy-start | bytes 49156
  863.4 342.3 %reduce-scatter.6.cloned.1.call-start = ((), (), s32[]{:S(2)}) async-start(), calls=%async_computation.7 | async-start | bytes 2359296 | tf_op jit(solution)/shard_map/reduce_scatter | solution.py:170
  947.1 260.4 %reduce-scatter.14.cloned.1.call-start = ((), (), s32[]{:S(2)}) async-start(), calls=%async_computation.11 | async-start | bytes 9437184 | tf_op jit(solution)/shard_map/reduce_scatter | solution.py:205
  989.7 220.5 %reduce-scatter.12.cloned.1.call-start = ((), (), s32[]{:S(2)}) async-start(), calls=%async_computation.10 | async-start | bytes 9437184 | tf_op jit(solution)/shard_map/reduce_scatter | solution.py:173
  1025.4 684.0 %all-reduce.21.cloned.1.call-start = ((), (), s32[]{:S(2)}) async-start(), calls=%async_computation.12 | async-start | bytes 33554432 | tf_op jit(solution)/shard_map/psum | solution.py:68
  1058.0 26.9 %copy-start.27 = (bf16[1024,512]{0,1:T(8,128)(2,1)S(1)}, bf16[1024,512]{0,1:T(8,128)(2,1)}, u32[]{:S(2)}) copy-start(bf16[1024,512]{0,1:T(8,128)(2,1)} %copy-done.26) | copy-start | bytes 3145732
  1058.0 26.9 %copy-start.36 = (f32[4,1024]{1,0:T(4,128)S(1)}, f32[4,1024]{1,0:T(4,128)}, u32[]{:S(2)}) copy-start(f32[4,1024]{1,0:T(4,128)} %copy-done.35) | copy-start | bytes 49156
  1143.3 52.0 %copy-start.73 = (f32[128,4]{0,1:T(4,128)S(1)}, f32[128,4]{0,1:T(4,128)}, u32[]{:S(2)}) copy-start(f32[128,4]{0,1:T(4,128)} %get-tuple-element.78) | copy-start | bytes 6148
  1143.3 52.0 %copy-start.74 = (f32[128,4]{0,1:T(4,128)S(1)}, f32[128,4]{0,1:T(4,128)}, u32[]{:S(2)}) copy-start(f32[128,4]{0,1:T(4,128)} %get-tuple-element.76) | copy-start | bytes 6148
  1143.3 52.0 %copy-start.55 = (f32[2048]{0:T(1024)S(1)}, f32[2048]{0:T(1024)}, u32[]{:S(2)}) copy-start(f32[2048]{0:T(1024)} %get-tuple-element.41) | copy-start | bytes 24580
  1143.3 52.0 %copy-start.56 = (f32[2048]{0:T(1024)S(1)}, f32[2048]{0:T(1024)}, u32[]{:S(2)}) copy-start(f32[2048]{0:T(1024)} %get-tuple-element.42) | copy-start | bytes 24580
  1143.3 52.0 %copy-start.57 = (f32[2048]{0:T(1024)S(1)}, f32[2048]{0:T(1024)}, u32[]{:S(2)}) copy-start(f32[2048]{0:T(1024)} %get-tuple-element.18) | copy-start | bytes 24580
  1143.3 52.0 %copy-start.58 = (f32[2048]{0:T(1024)S(1)}, f32[2048]{0:T(1024)}, u32[]{:S(2)}) copy-start(f32[2048]{0:T(1024)} %get-tuple-element.25) | copy-start | bytes 24580
  1143.4 52.0 %copy-start.59 = (f32[2048]{0:T(1024)S(1)}, f32[2048]{0:T(1024)}, u32[]{:S(2)}) copy-start(f32[2048]{0:T(1024)} %get-tuple-element.60) | copy-start | bytes 24580
  1143.4 52.0 %copy-start.60 = (f32[2048]{0:T(1024)S(1)}, f32[2048]{0:T(1024)}, u32[]{:S(2)}) copy-start(f32[2048]{0:T(1024)} %get-tuple-element.62) | copy-start | bytes 24580
  1143.4 706.0 %reduce-scatter.8.cloned.1.call-start = ((), (), s32[]{:S(2)}) async-start(), calls=%async_computation.8 | async-start | bytes 2162688 | tf_op jit(solution)/shard_map/reduce_scatter | solution.py:210
  1199.0 510.4 %copy-start.34 = (f32[2048]{0:T(1024)S(1)}, f32[2048]{0:T(1024)}, u32[]{:S(2)}) copy-start(f32[2048]{0:T(1024)} %copy-done.33) | copy-start | bytes 24580
  1199.0 510.4 %copy-start.40 = (f32[1024]{0:T(1024)S(1)}, f32[1024]{0:T(1024)}, u32[]{:S(2)}) copy-start(f32[1024]{0:T(1024)} %copy-done.39) | copy-start | bytes 12292
  1199.0 510.4 %copy-start.42 = (f32[1024]{0:T(1024)S(1)}, f32[1024]{0:T(1024)}, u32[]{:S(2)}) copy-start(f32[1024]{0:T(1024)} %copy-done.41) | copy-start | bytes 12292
  1791.8 57.5 %copy-start.1 = (bf16[512,2048]{1,0:T(8,128)(2,1)S(1)}, bf16[512,2048]{1,0:T(8,128)(2,1)}, u32[]{:S(2)}) copy-start(bf16[512,2048]{1,0:T(8,128)(2,1)} %param.25) | copy-start | bytes 6291460
  (73 other events, 593.2 us)
Sparse Core Ops, SparseCore 0:
  53.2 157.6 all-reduce.16
  254.4 153.9 all-reduce.18
  519.6 290.5 all-reduce.22
  863.5 40.2 reduce-scatter.9
  947.3 40.2 reduce-scatter.5
  990.9 71.2 reduce-scatter.13
  1066.0 71.2 reduce-scatter.11
  1143.4 565.9 all-reduce.20
  1712.2 137.0 reduce-scatter.7
where the time goes:
time: 1870 us; the launch traced here: 1860 us
  waiting for transfers between devices  1150 us (61%)
  matrix products  441 us (24%)
  other arithmetic  170 us (9%)
  blocking collectives  68.7 us (4%)
    psum x1, waiting for transfers between devices, forward_block(): summed = lax.psum(down_part.astype(jnp.bfloat16), 'tp').astype(jnp.float32)  496 us
    psum x2, waiting for transfers between devices, forward_block(): lax.psum(partial_value.astype(jnp.bfloat16), 'tp').astype(jnp.float32)  311 us
    psum x1, waiting for transfers between devices, backward_block(): lax.psum(partial2.astype(jnp.bfloat16), 'tp').astype(jnp.float32)  290 us
    unnamed x2, blocking collectives  68.7 us
    dot_general x2, matrix products, backward_block(): jnp.einsum('hst,shd->td', grad_scores, heads_q, preferred_element_type=jn...  51.7 us
    dot_general x2, matrix products, backward_block(): jnp.einsum('hst,td->shd', grad_scores, keys_low, preferred_element_type=j...  50.1 us
    reduce_sum x4, other arithmetic, layer_norm(): return center * lax.rsqrt(spread + 1e-05) * gain_vec + shift_vec  49.5 us
    reduce_scatter x1, waiting for transfers between devices, reduce_once(): lax.psum_scatter(grad_terms[12], ('dp', 'tp'), scatter_dimension=0, tiled...  48.8 us
  transfers between devices with their start and end apart: 9, of which 5 were waited for; matrix products, arithmetic and copies ran while one was open for 20% of the time, Pallas kernels for 0%

commit v1 on v0

--- a/solution.py
+++ b/solution.py
@@ -65,7 +65,9 @@
     )
     activated = gelu_tanh(before).astype(jnp.bfloat16)
     down_part = jnp.dot(activated, params["down_weight"], preferred_element_type=jnp.float32)
-    summed = lax.psum(down_part.astype(jnp.bfloat16), "tp").astype(jnp.float32)
+    summed = jnp.sum(lax.all_gather(down_part.astype(jnp.bfloat16), "tp"), axis=0).astype(
+        jnp.float32
+    )
     result = hidden1 + summed + params["down_bias"]
     kept_state = (
         normed1,

time: 1870 us -> 2010 us (1.075)
  waiting for transfers between devices: 1150 us -> 1260 us
  other arithmetic: 170 us -> 196 us
    all_gather x0 -> x2, waiting for transfers between devices: none -> 380 us  [forward_block(): lax.all_gather(down_part.astype(jnp.bfloat16), 'tp')]
    psum x1, waiting for transfers between devices: 496 us -> 228 us  [backward_block(): lax.psum(partial1.astype(jnp.bfloat16), 'tp').astype(jnp.float32)]
    reduce_sum x0 -> x2, other arithmetic: none -> 25.7 us  [forward_block(): jnp.sum(lax.all_gather(down_part.astype(jnp.bfloat16), 'tp'), axis=0)]
  transfers between devices with their start and end apart: 9 -> 11, of which waited for: 5 -> 7; matrix products, arithmetic and copies ran while one was open for 20% -> 25% of each run, Pallas kernels for 0% -> 0%
where the time goes in v1:
time: 2010 us; the launch traced here: 2000 us
  waiting for transfers between devices  1260 us (63%)
  matrix products  441 us (22%)
  other arithmetic  196 us (10%)
  blocking collectives  69.3 us (3%)
    all_gather x2, waiting for transfers between devices, forward_block(): lax.all_gather(down_part.astype(jnp.bfloat16), 'tp')  380 us
    psum x2, waiting for transfers between devices, forward_block(): lax.psum(partial_value.astype(jnp.bfloat16), 'tp').astype(jnp.float32)  311 us
    psum x1, waiting for transfers between devices, backward_block(): lax.psum(partial2.astype(jnp.bfloat16), 'tp').astype(jnp.float32)  280 us
    psum x1, waiting for transfers between devices, backward_block(): lax.psum(partial1.astype(jnp.bfloat16), 'tp').astype(jnp.float32)  228 us
    unnamed x2, blocking collectives  69.3 us
    reduce_scatter x1, waiting for transfers between devices, reduce_once(): lax.psum_scatter(grad_terms[12], ('dp', 'tp'), scatter_dimension=0, tiled...  63.5 us
    dot_general x2, matrix products, backward_block(): jnp.einsum('hst,td->shd', grad_scores, keys_low, preferred_element_type=j...  55.1 us
    reduce_sum x4, other arithmetic, layer_norm(): return center * lax.rsqrt(spread + 1e-05) * gain_vec + shift_vec  51.7 us
  transfers between devices with their start and end apart: 11, of which 7 were waited for; matrix products, arithmetic and copies ran while one was open for 25% of the time, Pallas kernels for 0%

profile of v1, /device:TPU:0, one launch (start us, length us, event | category | flops | bytes accessed | tf_op | source)
XLA Modules:
  0.0 2003.5 jit_solution(3909376264718276176)
XLA Ops:
  53.8 157.1 %all-reduce.17.cloned.1.call-done = bf16[1024,2048]{1,0:T(8,128)(2,1)} async-done(((bf16[1024,2048]{1,0:T(8,128)(2,1)}), bf16[1024,2048]{1,0:T(8,128)(2,1)}) %all-reduce.17.cloned.1.call-update) | async-done | bytes 4194320 | tf_op jit(solution)/shard_map/psum | solution.py:59
  241.0 17.0 fusion.100
  263.7 154.0 %all-reduce.19.cloned.1.call-done = bf16[1024,2048]{1,0:T(8,128)(2,1)} async-done(((bf16[1024,2048]{1,0:T(8,128)(2,1)}), bf16[1024,2048]{1,0:T(8,128)(2,1)}) %all-reduce.19.cloned.1.call-update) | async-done | bytes 4194320 | tf_op jit(solution)/shard_map/psum | solution.py:59
  430.7 13.1 fusion.162
  447.3 11.2 convolution_convert_fusion.2
  458.7 14.4 fusion.161
  476.8 14.5 convolution_convert_fusion.4
  491.4 19.6 convert_reduce_fusion.8
  513.0 13.5 convolution_convert_fusion
  526.4 20.9 %convert_reduce_fusion.9 = (f32[2048]{0:T(1024)}, bf16[1024,2048]{1,0:T(8,128)(2,1)}) fusion(f32[1024,2048]{1,0:T(8,128)} %copy-done.93, f32[2048]{0:T(1024)S(1)} %convert_element_type.321, bf16[2048,2048]{1,0:T(8,128)(2,1)} %param.31, bf16[2048,2048]{1,0:T(8,128)(2,1)} %param.33), kind=kOutput, calls=%fused_computation.107 | convolution fusion | flops 8638167040 | bytes 25182208 | tf_op jit(solution)/shard_map/dot_general | solution.py:106
  547.3 12.0 convolution_convert_fusion.1
  559.4 20.4 %fusion.85 = f32[2048,2048]{1,0:T(8,128)} fusion(bf16[2048,2048]{1,0:T(8,128)(2,1)} %param.33, f32[1024,2048]{1,0:T(8,128)} %copy-done.93, f32[2048]{0:T(1024)S(1)} %convert_element_type.321), kind=kOutput, calls=%fused_computation.150 | convolution fusion | flops 8610906112 | bytes 29368320 | tf_op jit(solution)/shard_map/dot_general | solution.py:105
  579.8 21.9 %add_convert_fusion = bf16[2048,2048]{1,0:T(8,128)(2,1)} fusion(f32[2048,2048]{1,0:T(8,128)} %fusion.85, bf16[2048,2048]{1,0:T(8,128)(2,1)} %param.33, f32[1024,2048]{1,0:T(8,128)} %copy-done.92, f32[2048]{0:T(1024)S(1)} %convert_element_type.321), kind=kOutput, calls=%fused_computation.14 | convolution fusion | flops 8619294720 | bytes 37756928 | tf_op jit(solution)/shard_map/dot_general | solution.py:105
  602.4 17.4 fusion.160
  619.8 17.6 add_convert_fusion.1
  638.3 106.2 %all-gather.7.cloned.1.call-done = bf16[4096,2048]{1,0:T(8,128)(2,1)} async-done(((bf16[1024,2048]{1,0:T(8,128)(2,1)}), bf16[4096,2048]{1,0:T(8,128)(2,1)}) %all-gather.7.cloned.1.call-update) | async-done | bytes 16777232 | tf_op jit(solution)/shard_map/all_gather | solution.py:68
  744.5 13.0 reduce_sum.379
  757.5 273.4 %all-gather.5.cloned.1.call-done = bf16[4096,2048]{1,0:T(8,128)(2,1)} async-done(((bf16[1024,2048]{1,0:T(8,128)(2,1)}), bf16[4096,2048]{1,0:T(8,128)(2,1)}) %all-gather.5.cloned.1.call-update) | async-done | bytes 16777232 | tf_op jit(solution)/shard_map/all_gather | solution.py:68
  1030.9 12.7 reduce_sum.370
  1043.6 279.5 %all-reduce.23.cloned.1.call-done = (bf16[1024,2048]{1,0:T(8,128)(2,1)}, bf16[1024,2048]{1,0:T(8,128)(2,1)}) async-done(((bf16[1024,2048]{1,0:T(8,128)(2,1)}, bf16[1024,2048]{1,0:T(8,128)(2,1)}), (bf16[1024,2048]{1,0:T(8,128)(2,1)}, bf16[1024,2048]{1,0:T(8,128)(2,1)})) %all-reduce.23.cloned.1.call-update) | async-done | bytes 8388624 | tf_op jit(solution)/shard_map/psum | solution.py:111
  1323.2 17.7 fusion.33
  1343.9 13.9 fusion.54
  1357.8 13.8 fusion.168
  1403.5 29.3 %convert_reduce_fusion.10 = (f32[128,4]{0,1:T(4,128)S(1)}, bf16[128,4,1024]{2,0,1:T(8,128)(2,1)}) fusion(f32[1024,1024,4]{1,0,2:T(8,128)} %fusion.135, f32[4,1024,1024]{1,2,0:T(8,128)} %get-tuple-element.71, f32[4,1024]{1,0:T(4,128)S(1)} %log_add_fusion, f32[1024,256]{1,0:T(8,128)S(1)} %copy-done.30), kind=kOutput, calls=%fused_computation.155 | convolution fusion | flops 1104679424 | bytes 68454400 | tf_op jit(solution)/shard_map/hst,td->shd/dot_general | solution.py:133
  1432.8 25.8 %convert_reduce_fusion.11 = (f32[128,4]{0,1:T(4,128)S(1)}, bf16[128,4,1024]{2,0,1:T(8,128)(2,1)}) fusion(f32[1024,1024,4]{1,0,2:T(8,128)} %fusion.138, f32[4,1024,1024]{1,2,0:T(8,128)} %get-tuple-element.69, f32[4,1024]{1,0:T(4,128)S(1)} %log_add_fusion.1, f32[1024,256]{1,0:T(8,128)} %copy-done.27), kind=kOutput, calls=%fused_computation.156 | convolution fusion | flops 1104679424 | bytes 68454400 | tf_op jit(solution)/shard_map/hst,td->shd/dot_general | solution.py:133
  1458.6 23.1 %fusion.123 = bf16[1024,128]{0,1:T(8,128)(2,1)S(1)} fusion(bf16[1024,4,128]{0,2,1:T(8,128)(2,1)S(1)} %bitcast.210, f32[1024,1024,4]{1,0,2:T(8,128)} %fusion.135, f32[4,1024,1024]{1,2,0:T(8,128)} %get-tuple-element.71, f32[4,1024]{1,0:T(4,128)S(1)} %log_add_fusion), kind=kOutput, calls=%fused_computation.179 | convolution fusion | flops 1103238144 | bytes 34881536 | tf_op jit(solution)/shard_map/hst,shd->td/dot_general | solution.py:137
  1502.2 23.9 %fusion.122 = bf16[1024,128]{0,1:T(8,128)(2,1)} fusion(bf16[1024,4,128]{0,2,1:T(8,128)(2,1)S(1)} %bitcast.208, f32[1024,1024,4]{1,0,2:T(8,128)} %fusion.138, f32[4,1024,1024]{1,2,0:T(8,128)} %get-tuple-element.69, f32[4,1024]{1,0:T(4,128)S(1)} %log_add_fusion.1), kind=kOutput, calls=%fused_computation.178 | convolution fusion | flops 1103238144 | bytes 34881536 | tf_op jit(solution)/shard_map/hst,shd->td/dot_general | solution.py:137
  1563.9 43.4 %all-reduce.3 = f32[128]{0:T(128)S(1)} all-reduce(f32[128]{0:T(128)S(1)} %add.339), channel_id=9, replica_groups=mesh['dp'=8,'tp'=4] {'dp','tp'}, use_global_device_ids=true, to_apply=%region_43.44.clone | all-reduce | flops 128 | bytes 1024
  1628.8 227.8 %all-reduce.21.cloned.1.call-done = (bf16[1024,2048]{1,0:T(8,128)(2,1)}, bf16[1024,2048]{1,0:T(8,128)(2,1)}) async-done(((bf16[1024,2048]{1,0:T(8,128)(2,1)}, bf16[1024,2048]{1,0:T(8,128)(2,1)}), (bf16[1024,2048]{1,0:T(8,128)(2,1)}, bf16[1024,2048]{1,0:T(8,128)(2,1)})) %all-reduce.21.cloned.1.call-update) | async-done | bytes 8388624 | tf_op jit(solution)/shard_map/psum | solution.py:147
  1876.9 25.8 %all-reduce.9 = (bf16[2048]{0:T(1024)(128)(2,1)S(1)}, bf16[2048]{0:T(1024)(128)(2,1)S(1)}, bf16[512]{0:T(512)(128)(2,1)S(1)}, bf16[2048]{0:T(1024)(128)(2,1)S(1)...) all-reduce(bf16[2048]{0:T(1024)(128)(2,1)S(1)} %add_convert_fusion., ...), channel_id=4, replica_groups=mesh['dp'=8,'tp'=4] {'dp'}, use_global_device_ids=true, to_apply=%region_32.33.clone | all-reduce | flops 14848 | bytes 59392
  1907.7 16.7 add_convert_fusion.4
  1933.0 63.5 %reduce-scatter.8.cloned.1.call-done = f32[64,256]{1,0:T(8,128)} async-done(((f32[2048,256]{1,0:T(8,128)}), f32[64,256]{1,0:T(8,128)}) %reduce-scatter.8.cloned.1.call-update) | async-done | bytes 65552 | tf_op jit(solution)/shard_map/reduce_scatter | solution.py:212
  (340 shorter events, 251.9 us)
Async XLA Ops:
  7.2 41.5 %copy-start = (bf16[512,2048]{1,0:T(8,128)(2,1)S(1)}, bf16[512,2048]{1,0:T(8,128)(2,1)}, u32[]{:S(2)}) copy-start(bf16[512,2048]{1,0:T(8,128)(2,1)} %param.25) | copy-start | bytes 6291460
  7.2 203.8 %all-reduce.17.cloned.1.call-start = ((), (), s32[]{:S(2)}) async-start(), calls=%async_computation.5 | async-start | bytes 8388608 | tf_op jit(solution)/shard_map/psum | solution.py:59
  8.1 232.9 %copy-start.80 = (f32[128]{0:T(128)}, f32[128]{0:T(128)S(1)}, u32[]{:S(2)}) copy-start(f32[128]{0:T(128)S(1)} %convert_element_type.308) | copy-start | bytes 1540
  13.0 204.2 %copy-start.33 = (f32[2048]{0:T(1024)}, f32[2048]{0:T(1024)S(1)}, u32[]{:S(2)}) copy-start(f32[2048]{0:T(1024)S(1)} %convert_element_type.305) | copy-start | bytes 24580
  53.1 364.5 %all-reduce.19.cloned.1.call-start = ((), (), s32[]{:S(2)}) async-start(), calls=%async_computation.6 | async-start | bytes 8388608 | tf_op jit(solution)/shard_map/psum | solution.py:59
  53.2 405.4 %copy-start.31 = (f32[2048]{0:T(1024)}, f32[2048]{0:T(1024)S(1)}, u32[]{:S(2)}) copy-start(f32[2048]{0:T(1024)S(1)} %convert_element_type.317) | copy-start | bytes 24580
  53.2 168.5 %copy-start.38 = (f32[1024]{0:T(1024)}, f32[1024]{0:T(1024)S(1)}, u32[]{:S(2)}) copy-start(f32[1024]{0:T(1024)S(1)} %broadcast_multiply_fusion.1) | copy-start | bytes 12292
  263.5 481.0 %all-gather.7.cloned.1.call-start = ((), (), s32[]{:S(2)}) async-start(), calls=%async_computation.13 | async-start | bytes 20971520 | tf_op jit(solution)/shard_map/all_gather | solution.py:68
  263.6 195.1 %copy-start.44 = (f32[2048]{0:T(1024)}, f32[2048]{0:T(1024)S(1)}, u32[]{:S(2)}) copy-start(f32[2048]{0:T(1024)S(1)} %convert_element_type.318) | copy-start | bytes 24580
  263.6 195.0 %copy-start.70 = (f32[2048]{0:T(1024)}, f32[2048]{0:T(1024)S(1)}, u32[]{:S(2)}) copy-start(f32[2048]{0:T(1024)S(1)} %convert_element_type.319) | copy-start | bytes 24580
  263.6 195.0 %copy-start.48 = (f32[1024]{0:T(1024)}, f32[1024]{0:T(1024)S(1)}, u32[]{:S(2)}) copy-start(f32[1024]{0:T(1024)S(1)} %broadcast_multiply_fusion.2) | copy-start | bytes 12292
  426.4 32.2 %copy-start.68 = (f32[1024]{0:T(1024)}, f32[1024]{0:T(1024)S(1)}, u32[]{:S(2)}) copy-start(f32[1024]{0:T(1024)S(1)} %get-tuple-element.32) | copy-start | bytes 12292
  426.5 20.8 %slice-start.10 = ((s8[8388608]{0:T(1024)(128)(4,1)}), s8[4194304]{0:T(1024)(128)(4,1)S(1)}, s32[]{:S(2)}) async-start(s8[8388608]{0:T(1024)(128)(4,1)} %bitcast.213), calls=%async_computation.26 | async-start | bytes 8388608
  458.6 572.4 %all-gather.5.cloned.1.call-start = ((), (), s32[]{:S(2)}) async-start(), calls=%async_computation.12 | async-start | bytes 20971520 | tf_op jit(solution)/shard_map/all_gather | solution.py:68
  491.3 831.8 %all-reduce.23.cloned.1.call-start = ((), (), s32[]{:S(2)}) async-start(), calls=%async_computation.15 | async-start | bytes 16777216 | tf_op jit(solution)/shard_map/psum | solution.py:111
  513.0 34.3 %slice-start.12 = ((s8[8388608]{0:T(1024)(128)(4,1)}), s8[4194304]{0:T(1024)(128)(4,1)S(1)}, s32[]{:S(2)}) async-start(s8[8388608]{0:T(1024)(128)(4,1)} %bitcast.215), calls=%async_computation.28 | async-start | bytes 8388608
  526.4 20.9 %slice-start.13 = ((s8[8388608]{0:T(1024)(128)(4,1)}), s8[4194304]{0:T(1024)(128)(4,1)S(1)}, s32[]{:S(2)}) async-start(s8[8388608]{0:T(1024)(128)(4,1)} %bitcast.215), calls=%async_computation.29 | async-start | bytes 8388608
  559.4 999.0 %reduce-scatter.14.cloned.1.call-start = ((), (), s32[]{:S(2)}) async-start(), calls=%async_computation.11 | async-start | bytes 9437184 | tf_op jit(solution)/shard_map/reduce_scatter | solution.py:207
  601.7 959.4 %reduce-scatter.12.cloned.1.call-start = ((), (), s32[]{:S(2)}) async-start(), calls=%async_computation.10 | async-start | bytes 9437184 | tf_op jit(solution)/shard_map/reduce_scatter | solution.py:175
  637.5 987.6 %reduce-scatter.10.cloned.1.call-start = ((), (), s32[]{:S(2)}) async-start(), calls=%async_computation.9 | async-start | bytes 2359296 | tf_op jit(solution)/shard_map/reduce_scatter | solution.py:204
  1323.2 20.7 %copy-start.13 = (bf16[1024,2048]{1,0:T(8,128)(2,1)S(1)}, bf16[1024,2048]{1,0:T(8,128)(2,1)}, u32[]{:S(2)}) copy-start(bf16[1024,2048]{1,0:T(8,128)(2,1)} %reduce_sum.379) | copy-start | bytes 12582916
  1323.2 34.7 %slice-start = ((s8[8388608]{0:T(1024)(128)(4,1)}), s8[4194304]{0:T(1024)(128)(4,1)S(1)}, s32[]{:S(2)}) async-start(s8[8388608]{0:T(1024)(128)(4,1)} %bitcast.193), calls=%async_computation.16 | async-start | bytes 8388608
  1403.5 223.5 %reduce-scatter.6.cloned.1.call-start = ((), (), s32[]{:S(2)}) async-start(), calls=%async_computation.7 | async-start | bytes 2359296 | tf_op jit(solution)/shard_map/reduce_scatter | solution.py:172
  1432.8 25.8 %copy-start.24 = (bf16[1024,512]{0,1:T(8,128)(2,1)S(1)}, bf16[1024,512]{0,1:T(8,128)(2,1)}, u32[]{:S(2)}) copy-start(bf16[1024,512]{0,1:T(8,128)(2,1)} %copy-done.23) | copy-start | bytes 3145732
  1481.7 54.4 %copy-start.25 = (bf16[1024,128]{0,1:T(8,128)(2,1)}, bf16[1024,128]{0,1:T(8,128)(2,1)S(1)}, u32[]{:S(2)}) copy-start(bf16[1024,128]{0,1:T(8,128)(2,1)S(1)} %fusion.123) | copy-start | bytes 786436
  1502.1 354.5 %all-reduce.21.cloned.1.call-start = ((), (), s32[]{:S(2)}) async-start(), calls=%async_computation.14 | async-start | bytes 16777216 | tf_op jit(solution)/shard_map/psum | solution.py:147
  1551.9 56.1 %copy-start.35 = (bf16[1024,128]{0,1:T(8,128)(2,1)S(1)}, bf16[1024,128]{0,1:T(8,128)(2,1)}, u32[]{:S(2)}) copy-start(bf16[1024,128]{0,1:T(8,128)(2,1)} %fusion.122) | copy-start | bytes 786436
  1551.9 444.6 %reduce-scatter.8.cloned.1.call-start = ((), (), s32[]{:S(2)}) async-start(), calls=%async_computation.8 | async-start | bytes 2162688 | tf_op jit(solution)/shard_map/reduce_scatter | solution.py:212
  1558.3 53.2 %copy-start.26 = (bf16[1024,128]{0,1:T(8,128)(2,1)S(1)}, bf16[1024,128]{0,1:T(8,128)(2,1)}, u32[]{:S(2)}) copy-start(bf16[1024,128]{0,1:T(8,128)(2,1)} %copy-done.25) | copy-start | bytes 786436
  1616.6 240.0 %copy-start.34 = (f32[2048]{0:T(1024)S(1)}, f32[2048]{0:T(1024)}, u32[]{:S(2)}) copy-start(f32[2048]{0:T(1024)} %copy-done.33) | copy-start | bytes 24580
  1616.6 240.0 %copy-start.37 = (f32[1024]{0:T(1024)S(1)}, f32[1024]{0:T(1024)}, u32[]{:S(2)}) copy-start(f32[1024]{0:T(1024)} %copy-done.36) | copy-start | bytes 12292
  1616.6 240.0 %copy-start.39 = (f32[1024]{0:T(1024)S(1)}, f32[1024]{0:T(1024)}, u32[]{:S(2)}) copy-start(f32[1024]{0:T(1024)} %copy-done.38) | copy-start | bytes 12292
  (88 other events, 731.7 us)
Sparse Core Ops, SparseCore 0:
  53.2 157.6 all-reduce.16
  263.6 153.9 all-reduce.18
  458.7 285.7 all-gather.6
  745.9 284.9 all-gather.4
  1033.4 289.7 all-reduce.22
  1326.4 70.2 reduce-scatter.13
  1400.6 71.2 reduce-scatter.11
  1475.2 41.3 reduce-scatter.9
  1520.3 41.2 reduce-scatter.5
  1564.0 292.5 all-reduce.20
  1859.4 137.0 reduce-scatter.7
